TPU v7x, 512 devices: a whole 4x4x16 slice. The times are simulated.
512 devices in a mesh: blk: 16 (over y_hi, x, core), dom: 32 (over y_lo, z).
Axes of the slice: x: 4, y: 4 (y_hi: 2, y_lo: 2; y = y_hi * 2 + y_lo), z: 16, core: 2. Of those that a mesh axis runs over, the one named last changes fastest.
Arguments:
- nodes: bfloat16 [65536, 512], P(('blk', 'dom')), may hold values from -6 to 6
- experts_list: int32 [512, 4], P(('blk', 'dom')), may hold values from 0 to 15, all different within a row
- w_query: bfloat16 [512, 512], replicated
- w_key: bfloat16 [512, 512], replicated
- w_value: bfloat16 [512, 512], replicated, may hold values from -0.25 to 0.25
- w_out: bfloat16 [512, 512], replicated, may hold values from -0.25 to 0.25
- w_up: bfloat16 [512, 1024], replicated, may hold values from -0.25 to 0.25
- w_down: bfloat16 [1024, 512], replicated, may hold values from -0.1875 to 0.1875
- cotangent: bfloat16 [65536, 512], P(('blk', 'dom')), may hold values from -6 to 6
Outputs:
- layer_out: bfloat16 [65536, 512], P(('blk', 'dom'))
- grad_nodes: bfloat16 [65536, 512], P(('blk', 'dom'))
Inputs may be any that keep to these rules, and one draw needn't show every extreme that they name: `experts_list`: row g names 4 different values; value c stands for the block held at blk index c and the same dom index as block g. Every value is named by some row.
All inputs are finite; a program needn't handle non-finite values.
Results may differ from a plain program's by a relative error of at most 0.0057.
Values may be sent and summed in bfloat16 or wider, within the bound.
A program may use at most 128 MiB of HBM per device.

v0:
```python
import jax
import jax.numpy as jnp
from jax import lax
from jax.sharding import PartitionSpec as P

H = 8
HEAD = 64
EPS = 1e-05
NEG = -1e30


def with_halo(array, sides, width):
    for axis, dim in sides:
        devices, length = (lax.axis_size(axis), array.shape[dim])
        up = [(i, (i + 1) % devices) for i in range(devices)]
        down = [(j, i) for i, j in up]
        last = lax.slice_in_dim(array, length - width, length, axis=dim)
        leading = lax.slice_in_dim(array, 0, width, axis=dim)
        before = lax.ppermute(last, axis, up)
        after = lax.ppermute(leading, axis, down)
        array = jnp.concatenate([before, array, after], axis=dim)
    return array


def shifted(array, axis, by):
    devices = lax.axis_size(axis)
    return lax.ppermute(array, axis, [(i, (i + by) % devices) for i in range(devices)])


def normalize(values):
    mean_v = jnp.mean(values, axis=-1, keepdims=True)
    centered = values - mean_v
    inv_std = lax.rsqrt(jnp.mean(centered * centered, axis=-1, keepdims=True) + EPS)
    return (centered * inv_std, inv_std)


def normalize_back(values, upstream):
    unit, inv_std = normalize(values)
    return inv_std * (
        upstream
        - jnp.mean(upstream, axis=-1, keepdims=True)
        - unit * jnp.mean(upstream * unit, axis=-1, keepdims=True)
    )


def heads_of(rows):
    return rows.reshape(rows.shape[0], H, HEAD)


def attend(queries, keyvals):
    width = queries.shape[1]
    scale = HEAD ** (-0.5)
    qh = heads_of(queries)
    kh = heads_of(keyvals[:, :width])
    vh = heads_of(keyvals[:, width:])
    scores = jnp.einsum("qhd,khd->hqk", qh, kh, preferred_element_type=jnp.float32) * scale
    top = jnp.max(scores, axis=-1, keepdims=True)
    weights = jnp.exp(scores - top)
    total = jnp.sum(weights, axis=-1, keepdims=True)
    mixed = jnp.einsum(
        "hqk,khd->qhd", weights.astype(jnp.bfloat16), vh, preferred_element_type=jnp.float32
    )
    mixed = mixed / jnp.transpose(total, (1, 0, 2))
    lse = (top + jnp.log(total))[..., 0]
    return (mixed.reshape(queries.shape[0], width).astype(jnp.bfloat16), lse)


def attend_back(queries, keyvals, grad_out, lse, delta, qmult):
    width = queries.shape[1]
    scale = HEAD ** (-0.5)
    qh = heads_of(queries)
    kh = heads_of(keyvals[:, :width])
    vh = heads_of(keyvals[:, width:])
    gh = heads_of(grad_out)
    scores = jnp.einsum("qhd,khd->hqk", qh, kh, preferred_element_type=jnp.float32) * scale
    valid = qmult[None, :, None] > 0
    scores = jnp.where(valid, scores, NEG)
    probs = jnp.exp(scores - lse[..., None]) * qmult[None, :, None]
    grad_v = jnp.einsum(
        "hqk,qhd->khd", probs.astype(jnp.bfloat16), gh, preferred_element_type=jnp.float32
    )
    dprob = jnp.einsum("qhd,khd->hqk", gh, vh, preferred_element_type=jnp.float32)
    dscore = (probs * (dprob - delta[..., None]) * scale).astype(jnp.bfloat16)
    grad_q = jnp.einsum("hqk,khd->qhd", dscore, kh, preferred_element_type=jnp.float32)
    grad_k = jnp.einsum("hqk,qhd->khd", dscore, qh, preferred_element_type=jnp.float32)
    count = keyvals.shape[0]
    return (
        grad_q.reshape(queries.shape[0], width),
        jnp.concatenate([grad_k.reshape(count, width), grad_v.reshape(count, width)], 1),
    )


def on_device(nodes, experts_list, w_query, w_key, w_value, w_out, w_up, w_down, cotangent):
    f32 = jnp.float32
    bf16 = jnp.bfloat16
    rows, width = nodes.shape
    groups = lax.axis_size("blk")
    place = lax.axis_index("blk")
    x_full = nodes.astype(f32)
    unit, _ = normalize(x_full)
    normed = unit.astype(bf16)
    queries = jnp.dot(normed, w_query, preferred_element_type=f32).astype(bf16)
    keys = jnp.dot(normed, w_key, preferred_element_type=f32).astype(bf16)
    values = jnp.dot(normed, w_value, preferred_element_type=f32).astype(bf16)
    keyvals = jnp.concatenate([keys, values], 1)
    window = with_halo(keyvals, (("dom", 0),), rows)
    panels = lax.all_gather(keyvals, "blk", axis=0, tiled=True)
    listed = experts_list[0]
    listed_count = listed.shape[0]
    chosen = jnp.take(panels.reshape(groups, rows, 2 * width), listed, axis=0)
    all_keys = jnp.concatenate([window, chosen.reshape(listed_count * rows, 2 * width)], 0)
    mixed, lse = attend(queries, all_keys)
    resid = x_full + jnp.dot(mixed, w_out, preferred_element_type=f32)
    unit2, _ = normalize(resid)
    normed2 = unit2.astype(bf16)
    pre = jnp.dot(normed2, w_up, preferred_element_type=f32)
    act, gelu_back = jax.vjp(jax.nn.gelu, pre)
    layer_out = (resid + jnp.dot(act.astype(bf16), w_down, preferred_element_type=f32)).astype(bf16)
    grad_act = jnp.dot(cotangent, w_down.T, preferred_element_type=f32)
    grad_pre = gelu_back(grad_act)[0].astype(bf16)
    grad_norm2 = jnp.dot(grad_pre, w_up.T, preferred_element_type=f32)
    grad_resid = cotangent.astype(f32) + normalize_back(resid, grad_norm2)
    grad_mixed = jnp.dot(grad_resid.astype(bf16), w_out.T, preferred_element_type=f32).astype(bf16)
    delta = jnp.sum(heads_of(grad_mixed).astype(f32) * heads_of(mixed).astype(f32), axis=-1).T
    ones_rows = jnp.ones((rows,), f32)
    grad_q, grad_kv = attend_back(queries, all_keys, grad_mixed, lse, delta, ones_rows)
    from_upper = shifted(grad_kv[:rows].astype(jnp.bfloat16), "dom", -1).astype(jnp.float32)
    from_lower = shifted(grad_kv[2 * rows : 3 * rows].astype(jnp.bfloat16), "dom", 1).astype(
        jnp.float32
    )
    own_grad = grad_kv[rows : 2 * rows] + from_upper + from_lower
    listed_parts = grad_kv[3 * rows :].reshape(listed_count, rows, 2 * width)
    onehot = (listed[:, None] == jnp.arange(groups, dtype=jnp.int32)[None, :]).astype(f32)
    far_parts = jnp.einsum("eg,erc->grc", onehot, listed_parts).reshape(groups * rows, 2 * width)

    def carry_step(step, running):
        running = shifted(running.astype(jnp.bfloat16), "blk", 1).astype(running.dtype)
        target = (place - step - 1) % groups
        return running + lax.dynamic_slice_in_dim(far_parts, target * rows, rows, 0)

    first = lax.dynamic_slice_in_dim(far_parts, (place - 1) % groups * rows, rows, 0)
    far_grad = lax.fori_loop(1, groups, carry_step, first)
    key_grad = own_grad + far_grad
    grad_in = (
        jnp.dot(grad_q.astype(bf16), w_query.T, preferred_element_type=f32)
        + jnp.dot(key_grad[:, :width].astype(bf16), w_key.T, preferred_element_type=f32)
        + jnp.dot(key_grad[:, width:].astype(bf16), w_value.T, preferred_element_type=f32)
    )
    grad_nodes = (grad_resid + normalize_back(x_full, grad_in)).astype(bf16)
    return (layer_out, grad_nodes)


def solution(mesh):
    return jax.shard_map(
        on_device,
        mesh=mesh,
        in_specs=(
            P(("blk", "dom"), None),
            P(("blk", "dom"), None),
            P(),
            P(),
            P(),
            P(),
            P(),
            P(),
            P(("blk", "dom"), None),
        ),
        out_specs=(P(("blk", "dom"), None), P(("blk", "dom"), None)),
        check_vma=False,
    )
```

profile of v0, /device:TPU:8, one launch (start us, length us, event | category | flops | bytes accessed | tf_op | source)
XLA Modules:
  0.0 364.6 jit_solution(6669680879408683189)
XLA Ops:
  13.0 11.3 %collective-permute-start.2 = (bf16[128,1024]{1,0:T(8,128)(2,1)}, bf16[128,1024]{1,0:T(8,128)(2,1)S(1)}, u32[]{:S(2)}, u32[]{:S(2)}) collective-permute-start(bf16[128,1024]{1,0:T(8,128)(2,1)} %pad_maximum_fusion.2), channel_id=1, source_target_pairs={{1,0},{2,1},{3,2},{4,3},{5,4},{6,5},{7,6},{8,7},{9,8},{10,9},{11,1... | collective-permute-start | bytes 786440 | tf_op jit(solution)/shard_map/ppermute | solution.py:20
  24.3 1.9 collective-permute-start.1
  31.8 4.5 %collective-permute-done.1 = bf16[128,1024]{1,0:T(8,128)(2,1)S(1)} collective-permute-done((bf16[128,1024]{1,0:T(8,128)(2,1)}, bf16[128,1024]{1,0:T(8,128)(2,1)S(1)}, u32[]{:S(2)}, u32[]{:S(2)}) %collective-permute-start.1) | collective-permute-done | bytes 262176 | tf_op jit(solution)/shard_map/ppermute | solution.py:19
  37.1 51.1 %all-gather.2.cloned.1.call-done = bf16[2048,1024]{1,0:T(8,128)(2,1)} async-done(((bf16[128,1024]{1,0:T(8,128)(2,1)}), bf16[2048,1024]{1,0:T(8,128)(2,1)}) %all-gather.2.cloned.1.call-update) | async-done | bytes 4194320 | tf_op jit(solution)/shard_map/all_gather | solution.py:107
  88.2 2.8 gather_fusion
  99.1 3.6 fusion.82
  103.9 2.1 convolution_convert_fusion.1
  108.0 3.3 multiply_convert_fusion
  113.8 2.1 fusion.7
  117.7 2.8 copy.27
  126.2 4.9 %copy.29 = f32[16,128,1024]{2,1,0:T(8,128)S(1)} copy(f32[16,128,1024]{2,0,1:T(8,128)S(1)} %fusion.5) | data formatting | bytes 16777216 | tf_op jit(solution)/shard_map/eg,erc->grc/dot_general | solution.py:134
  131.1 2.8 fusion.83
  133.9 3.4 collective-permute-start.4
  137.3 5.3 %collective-permute-start.3 = (bf16[128,1024]{1,0:T(8,128)(2,1)}, bf16[128,1024]{1,0:T(8,128)(2,1)}, u32[]{:S(2)}, u32[]{:S(2)}) collective-permute-start(bf16[128,1024]{1,0:T(8,128)(2,1)} %get-tuple-element.127), channel_id=1, source_target_pairs={{0,31},{1,0},{2,1},{3,2},{4,3},{5,4},{6,5},{7,6},{8,7},{9,8},{10,9... | collective-permute-start | bytes 786440 | tf_op jit(solution)/shard_map/ppermute | solution.py:27
  142.7 211.9 %while.15 = (s32[]{:T(128)}, f32[128,1024]{1,0:T(8,128)S(1)}, s32[]{:T(128)}, f32[2048,1024]{1,0:T(8,128)}, s32[]{:T(128)}, /*index=5*/s32[]{:T(128)}, s32[]{:T(...) while((s32[]{:T(128)}, f32[128,1024]{1,0:T(8,128)S(1)}, s32[]{:T(128)}, f32[2048,1024]{1,0:T(8,128)}, ...), condition=%wide.region_10.11_spmd, body=%wide.region_9.10_spmd.sunk | while | flops 393235 | bytes 4194664 | solution.py:142
  143.4 1.9 collective-permute-start
  145.4 9.6 %collective-permute-done = bf16[128,1024]{1,0:T(8,128)(2,1)S(1)} collective-permute-done((bf16[128,1024]{1,0:T(8,128)(2,1)}, bf16[128,1024]{1,0:T(8,128)(2,1)S(1)}, u32[]{:S(2)}, u32[]{:S(2)}) %collective-permute-start) | collective-permute-done | bytes 262176 | tf_op jit(solution)/shard_map/while/body/eval_jaxpr/ppermute | solution.py:27
  157.6 1.9 collective-permute-start
  159.5 9.6 %collective-permute-done = bf16[128,1024]{1,0:T(8,128)(2,1)S(1)} collective-permute-done((bf16[128,1024]{1,0:T(8,128)(2,1)}, bf16[128,1024]{1,0:T(8,128)(2,1)S(1)}, u32[]{:S(2)}, u32[]{:S(2)}) %collective-permute-start) | collective-permute-done | bytes 262176 | tf_op jit(solution)/shard_map/while/body/eval_jaxpr/ppermute | solution.py:27
  173.6 9.6 %collective-permute-done = bf16[128,1024]{1,0:T(8,128)(2,1)S(1)} collective-permute-done((bf16[128,1024]{1,0:T(8,128)(2,1)}, bf16[128,1024]{1,0:T(8,128)(2,1)S(1)}, u32[]{:S(2)}, u32[]{:S(2)}) %collective-permute-start) | collective-permute-done | bytes 262176 | tf_op jit(solution)/shard_map/while/body/eval_jaxpr/ppermute | solution.py:27
  187.8 9.6 %collective-permute-done = bf16[128,1024]{1,0:T(8,128)(2,1)S(1)} collective-permute-done((bf16[128,1024]{1,0:T(8,128)(2,1)}, bf16[128,1024]{1,0:T(8,128)(2,1)S(1)}, u32[]{:S(2)}, u32[]{:S(2)}) %collective-permute-start) | collective-permute-done | bytes 262176 | tf_op jit(solution)/shard_map/while/body/eval_jaxpr/ppermute | solution.py:27
  201.9 9.6 %collective-permute-done = bf16[128,1024]{1,0:T(8,128)(2,1)S(1)} collective-permute-done((bf16[128,1024]{1,0:T(8,128)(2,1)}, bf16[128,1024]{1,0:T(8,128)(2,1)S(1)}, u32[]{:S(2)}, u32[]{:S(2)}) %collective-permute-start) | collective-permute-done | bytes 262176 | tf_op jit(solution)/shard_map/while/body/eval_jaxpr/ppermute | solution.py:27
  216.0 9.6 %collective-permute-done = bf16[128,1024]{1,0:T(8,128)(2,1)S(1)} collective-permute-done((bf16[128,1024]{1,0:T(8,128)(2,1)}, bf16[128,1024]{1,0:T(8,128)(2,1)S(1)}, u32[]{:S(2)}, u32[]{:S(2)}) %collective-permute-start) | collective-permute-done | bytes 262176 | tf_op jit(solution)/shard_map/while/body/eval_jaxpr/ppermute | solution.py:27
  230.1 9.6 %collective-permute-done = bf16[128,1024]{1,0:T(8,128)(2,1)S(1)} collective-permute-done((bf16[128,1024]{1,0:T(8,128)(2,1)}, bf16[128,1024]{1,0:T(8,128)(2,1)S(1)}, u32[]{:S(2)}, u32[]{:S(2)}) %collective-permute-start) | collective-permute-done | bytes 262176 | tf_op jit(solution)/shard_map/while/body/eval_jaxpr/ppermute | solution.py:27
  244.3 9.6 %collective-permute-done = bf16[128,1024]{1,0:T(8,128)(2,1)S(1)} collective-permute-done((bf16[128,1024]{1,0:T(8,128)(2,1)}, bf16[128,1024]{1,0:T(8,128)(2,1)S(1)}, u32[]{:S(2)}, u32[]{:S(2)}) %collective-permute-start) | collective-permute-done | bytes 262176 | tf_op jit(solution)/shard_map/while/body/eval_jaxpr/ppermute | solution.py:27
  258.4 9.6 %collective-permute-done = bf16[128,1024]{1,0:T(8,128)(2,1)S(1)} collective-permute-done((bf16[128,1024]{1,0:T(8,128)(2,1)}, bf16[128,1024]{1,0:T(8,128)(2,1)S(1)}, u32[]{:S(2)}, u32[]{:S(2)}) %collective-permute-start) | collective-permute-done | bytes 262176 | tf_op jit(solution)/shard_map/while/body/eval_jaxpr/ppermute | solution.py:27
  272.5 9.6 %collective-permute-done = bf16[128,1024]{1,0:T(8,128)(2,1)S(1)} collective-permute-done((bf16[128,1024]{1,0:T(8,128)(2,1)}, bf16[128,1024]{1,0:T(8,128)(2,1)S(1)}, u32[]{:S(2)}, u32[]{:S(2)}) %collective-permute-start) | collective-permute-done | bytes 262176 | tf_op jit(solution)/shard_map/while/body/eval_jaxpr/ppermute | solution.py:27
  286.6 9.6 %collective-permute-done = bf16[128,1024]{1,0:T(8,128)(2,1)S(1)} collective-permute-done((bf16[128,1024]{1,0:T(8,128)(2,1)}, bf16[128,1024]{1,0:T(8,128)(2,1)S(1)}, u32[]{:S(2)}, u32[]{:S(2)}) %collective-permute-start) | collective-permute-done | bytes 262176 | tf_op jit(solution)/shard_map/while/body/eval_jaxpr/ppermute | solution.py:27
  300.8 9.6 %collective-permute-done = bf16[128,1024]{1,0:T(8,128)(2,1)S(1)} collective-permute-done((bf16[128,1024]{1,0:T(8,128)(2,1)}, bf16[128,1024]{1,0:T(8,128)(2,1)S(1)}, u32[]{:S(2)}, u32[]{:S(2)}) %collective-permute-start) | collective-permute-done | bytes 262176 | tf_op jit(solution)/shard_map/while/body/eval_jaxpr/ppermute | solution.py:27
  314.9 9.6 %collective-permute-done = bf16[128,1024]{1,0:T(8,128)(2,1)S(1)} collective-permute-done((bf16[128,1024]{1,0:T(8,128)(2,1)}, bf16[128,1024]{1,0:T(8,128)(2,1)S(1)}, u32[]{:S(2)}, u32[]{:S(2)}) %collective-permute-start) | collective-permute-done | bytes 262176 | tf_op jit(solution)/shard_map/while/body/eval_jaxpr/ppermute | solution.py:27
  329.0 9.6 %collective-permute-done = bf16[128,1024]{1,0:T(8,128)(2,1)S(1)} collective-permute-done((bf16[128,1024]{1,0:T(8,128)(2,1)}, bf16[128,1024]{1,0:T(8,128)(2,1)S(1)}, u32[]{:S(2)}, u32[]{:S(2)}) %collective-permute-start) | collective-permute-done | bytes 262176 | tf_op jit(solution)/shard_map/while/body/eval_jaxpr/ppermute | solution.py:27
  343.1 9.6 %collective-permute-done = bf16[128,1024]{1,0:T(8,128)(2,1)S(1)} collective-permute-done((bf16[128,1024]{1,0:T(8,128)(2,1)}, bf16[128,1024]{1,0:T(8,128)(2,1)S(1)}, u32[]{:S(2)}, u32[]{:S(2)}) %collective-permute-start) | collective-permute-done | bytes 262176 | tf_op jit(solution)/shard_map/while/body/eval_jaxpr/ppermute | solution.py:27
  (177 shorter events, 100.1 us)
Async XLA Ops:
  7.2 89.8 %copy-start = (bf16[512,1024]{1,0:T(8,128)(2,1)S(1)}, bf16[512,1024]{1,0:T(8,128)(2,1)}, u32[]{:S(2)}) copy-start(bf16[512,1024]{1,0:T(8,128)(2,1)} %param.17) | copy-start | bytes 3145732
  7.2 81.0 %all-gather.2.cloned.1.call-start = ((), (), s32[]{:S(2)}) async-start(), calls=%async_computation | async-start | bytes 4456448 | tf_op jit(solution)/shard_map/all_gather | solution.py:107
  13.0 18.0 %collective-permute-start.2 = (bf16[128,1024]{1,0:T(8,128)(2,1)}, bf16[128,1024]{1,0:T(8,128)(2,1)S(1)}, u32[]{:S(2)}, u32[]{:S(2)}) collective-permute-start(bf16[128,1024]{1,0:T(8,128)(2,1)} %pad_maximum_fusion.2), channel_id=1, source_target_pairs={{1,0},{2,1},{3,2},{4,3},{5,4},{6,5},{7,6},{8,7},{9,8},{10,9},{11,1... | collective-permute-start | bytes 786440 | tf_op jit(solution)/shard_map/ppermute | solution.py:20
  24.3 12.0 %collective-permute-start.1 = (bf16[128,1024]{1,0:T(8,128)(2,1)}, bf16[128,1024]{1,0:T(8,128)(2,1)S(1)}, u32[]{:S(2)}, u32[]{:S(2)}) collective-permute-start(bf16[128,1024]{1,0:T(8,128)(2,1)} %pad_maximum_fusion.2), channel_id=1, source_target_pairs={{0,1},{1,2},{2,3},{3,4},{4,5},{5,6},{6,7},{7,8},{8,9},{9,10},{10,1... | collective-permute-start | bytes 786440 | tf_op jit(solution)/shard_map/ppermute | solution.py:19
  94.8 3.3 copy-start.26
  95.8 3.3 copy-start.16
  96.2 7.2 %copy-start.7 = (f32[128,512]{1,0:T(8,128)}, f32[128,512]{1,0:T(8,128)S(1)}, u32[]{:S(2)}) copy-start(f32[128,512]{1,0:T(8,128)S(1)} %get-tuple-element.134) | copy-start | bytes 786436
  111.2 2.5 copy-start.2
  122.3 2.5 copy-start.25
  131.1 11.6 %copy-start.4 = (f32[16,128,1024]{2,1,0:T(8,128)}, f32[16,128,1024]{2,1,0:T(8,128)S(1)}, u32[]{:S(2)}) copy-start(f32[16,128,1024]{2,1,0:T(8,128)S(1)} %copy.29) | copy-start | bytes 25165828
  133.9 220.7 %collective-permute-start.4 = (bf16[128,1024]{1,0:T(8,128)(2,1)}, bf16[128,1024]{1,0:T(8,128)(2,1)}, u32[]{:S(2)}, u32[]{:S(2)}) collective-permute-start(bf16[128,1024]{1,0:T(8,128)(2,1)} %get-tuple-element.128), channel_id=1, source_target_pairs={{0,1},{1,2},{2,3},{3,4},{4,5},{5,6},{6,7},{7,8},{8,9},{9,10},{10,1... | collective-permute-start | bytes 786440 | tf_op jit(solution)/shard_map/ppermute | solution.py:27
  137.3 217.3 %collective-permute-start.3 = (bf16[128,1024]{1,0:T(8,128)(2,1)}, bf16[128,1024]{1,0:T(8,128)(2,1)}, u32[]{:S(2)}, u32[]{:S(2)}) collective-permute-start(bf16[128,1024]{1,0:T(8,128)(2,1)} %get-tuple-element.127), channel_id=1, source_target_pairs={{0,31},{1,0},{2,1},{3,2},{4,3},{5,4},{6,5},{7,6},{8,7},{9,8},{10,9... | collective-permute-start | bytes 786440 | tf_op jit(solution)/shard_map/ppermute | solution.py:27
  143.4 11.5 %collective-permute-start = (bf16[128,1024]{1,0:T(8,128)(2,1)}, bf16[128,1024]{1,0:T(8,128)(2,1)S(1)}, u32[]{:S(2)}, u32[]{:S(2)}) collective-permute-start(bf16[128,1024]{1,0:T(8,128)(2,1)} %convert_element_type.201), channel_id=1, source_target_pairs={{0,32},{32,64},{64,96},{96,128},{128,160},{160,192},{192,224},{224... | collective-permute-start | bytes 786440 | tf_op jit(solution)/shard_map/while/body/eval_jaxpr/ppermute | solution.py:27
  157.6 11.5 %collective-permute-start = (bf16[128,1024]{1,0:T(8,128)(2,1)}, bf16[128,1024]{1,0:T(8,128)(2,1)S(1)}, u32[]{:S(2)}, u32[]{:S(2)}) collective-permute-start(bf16[128,1024]{1,0:T(8,128)(2,1)} %convert_element_type.201), channel_id=1, source_target_pairs={{0,32},{32,64},{64,96},{96,128},{128,160},{160,192},{192,224},{224... | collective-permute-start | bytes 786440 | tf_op jit(solution)/shard_map/while/body/eval_jaxpr/ppermute | solution.py:27
  171.7 11.5 %collective-permute-start = (bf16[128,1024]{1,0:T(8,128)(2,1)}, bf16[128,1024]{1,0:T(8,128)(2,1)S(1)}, u32[]{:S(2)}, u32[]{:S(2)}) collective-permute-start(bf16[128,1024]{1,0:T(8,128)(2,1)} %convert_element_type.201), channel_id=1, source_target_pairs={{0,32},{32,64},{64,96},{96,128},{128,160},{160,192},{192,224},{224... | collective-permute-start | bytes 786440 | tf_op jit(solution)/shard_map/while/body/eval_jaxpr/ppermute | solution.py:27
  185.8 11.5 %collective-permute-start = (bf16[128,1024]{1,0:T(8,128)(2,1)}, bf16[128,1024]{1,0:T(8,128)(2,1)S(1)}, u32[]{:S(2)}, u32[]{:S(2)}) collective-permute-start(bf16[128,1024]{1,0:T(8,128)(2,1)} %convert_element_type.201), channel_id=1, source_target_pairs={{0,32},{32,64},{64,96},{96,128},{128,160},{160,192},{192,224},{224... | collective-permute-start | bytes 786440 | tf_op jit(solution)/shard_map/while/body/eval_jaxpr/ppermute | solution.py:27
  199.9 11.5 %collective-permute-start = (bf16[128,1024]{1,0:T(8,128)(2,1)}, bf16[128,1024]{1,0:T(8,128)(2,1)S(1)}, u32[]{:S(2)}, u32[]{:S(2)}) collective-permute-start(bf16[128,1024]{1,0:T(8,128)(2,1)} %convert_element_type.201), channel_id=1, source_target_pairs={{0,32},{32,64},{64,96},{96,128},{128,160},{160,192},{192,224},{224... | collective-permute-start | bytes 786440 | tf_op jit(solution)/shard_map/while/body/eval_jaxpr/ppermute | solution.py:27
  214.1 11.5 %collective-permute-start = (bf16[128,1024]{1,0:T(8,128)(2,1)}, bf16[128,1024]{1,0:T(8,128)(2,1)S(1)}, u32[]{:S(2)}, u32[]{:S(2)}) collective-permute-start(bf16[128,1024]{1,0:T(8,128)(2,1)} %convert_element_type.201), channel_id=1, source_target_pairs={{0,32},{32,64},{64,96},{96,128},{128,160},{160,192},{192,224},{224... | collective-permute-start | bytes 786440 | tf_op jit(solution)/shard_map/while/body/eval_jaxpr/ppermute | solution.py:27
  228.2 11.5 %collective-permute-start = (bf16[128,1024]{1,0:T(8,128)(2,1)}, bf16[128,1024]{1,0:T(8,128)(2,1)S(1)}, u32[]{:S(2)}, u32[]{:S(2)}) collective-permute-start(bf16[128,1024]{1,0:T(8,128)(2,1)} %convert_element_type.201), channel_id=1, source_target_pairs={{0,32},{32,64},{64,96},{96,128},{128,160},{160,192},{192,224},{224... | collective-permute-start | bytes 786440 | tf_op jit(solution)/shard_map/while/body/eval_jaxpr/ppermute | solution.py:27
  242.3 11.5 %collective-permute-start = (bf16[128,1024]{1,0:T(8,128)(2,1)}, bf16[128,1024]{1,0:T(8,128)(2,1)S(1)}, u32[]{:S(2)}, u32[]{:S(2)}) collective-permute-start(bf16[128,1024]{1,0:T(8,128)(2,1)} %convert_element_type.201), channel_id=1, source_target_pairs={{0,32},{32,64},{64,96},{96,128},{128,160},{160,192},{192,224},{224... | collective-permute-start | bytes 786440 | tf_op jit(solution)/shard_map/while/body/eval_jaxpr/ppermute | solution.py:27
  256.4 11.5 %collective-permute-start = (bf16[128,1024]{1,0:T(8,128)(2,1)}, bf16[128,1024]{1,0:T(8,128)(2,1)S(1)}, u32[]{:S(2)}, u32[]{:S(2)}) collective-permute-start(bf16[128,1024]{1,0:T(8,128)(2,1)} %convert_element_type.201), channel_id=1, source_target_pairs={{0,32},{32,64},{64,96},{96,128},{128,160},{160,192},{192,224},{224... | collective-permute-start | bytes 786440 | tf_op jit(solution)/shard_map/while/body/eval_jaxpr/ppermute | solution.py:27
  270.6 11.5 %collective-permute-start = (bf16[128,1024]{1,0:T(8,128)(2,1)}, bf16[128,1024]{1,0:T(8,128)(2,1)S(1)}, u32[]{:S(2)}, u32[]{:S(2)}) collective-permute-start(bf16[128,1024]{1,0:T(8,128)(2,1)} %convert_element_type.201), channel_id=1, source_target_pairs={{0,32},{32,64},{64,96},{96,128},{128,160},{160,192},{192,224},{224... | collective-permute-start | bytes 786440 | tf_op jit(solution)/shard_map/while/body/eval_jaxpr/ppermute | solution.py:27
  284.7 11.5 %collective-permute-start = (bf16[128,1024]{1,0:T(8,128)(2,1)}, bf16[128,1024]{1,0:T(8,128)(2,1)S(1)}, u32[]{:S(2)}, u32[]{:S(2)}) collective-permute-start(bf16[128,1024]{1,0:T(8,128)(2,1)} %convert_element_type.201), channel_id=1, source_target_pairs={{0,32},{32,64},{64,96},{96,128},{128,160},{160,192},{192,224},{224... | collective-permute-start | bytes 786440 | tf_op jit(solution)/shard_map/while/body/eval_jaxpr/ppermute | solution.py:27
  298.8 11.5 %collective-permute-start = (bf16[128,1024]{1,0:T(8,128)(2,1)}, bf16[128,1024]{1,0:T(8,128)(2,1)S(1)}, u32[]{:S(2)}, u32[]{:S(2)}) collective-permute-start(bf16[128,1024]{1,0:T(8,128)(2,1)} %convert_element_type.201), channel_id=1, source_target_pairs={{0,32},{32,64},{64,96},{96,128},{128,160},{160,192},{192,224},{224... | collective-permute-start | bytes 786440 | tf_op jit(solution)/shard_map/while/body/eval_jaxpr/ppermute | solution.py:27
  312.9 11.5 %collective-permute-start = (bf16[128,1024]{1,0:T(8,128)(2,1)}, bf16[128,1024]{1,0:T(8,128)(2,1)S(1)}, u32[]{:S(2)}, u32[]{:S(2)}) collective-permute-start(bf16[128,1024]{1,0:T(8,128)(2,1)} %convert_element_type.201), channel_id=1, source_target_pairs={{0,32},{32,64},{64,96},{96,128},{128,160},{160,192},{192,224},{224... | collective-permute-start | bytes 786440 | tf_op jit(solution)/shard_map/while/body/eval_jaxpr/ppermute | solution.py:27
  327.1 11.5 %collective-permute-start = (bf16[128,1024]{1,0:T(8,128)(2,1)}, bf16[128,1024]{1,0:T(8,128)(2,1)S(1)}, u32[]{:S(2)}, u32[]{:S(2)}) collective-permute-start(bf16[128,1024]{1,0:T(8,128)(2,1)} %convert_element_type.201), channel_id=1, source_target_pairs={{0,32},{32,64},{64,96},{96,128},{128,160},{160,192},{192,224},{224... | collective-permute-start | bytes 786440 | tf_op jit(solution)/shard_map/while/body/eval_jaxpr/ppermute | solution.py:27
  341.2 11.5 %collective-permute-start = (bf16[128,1024]{1,0:T(8,128)(2,1)}, bf16[128,1024]{1,0:T(8,128)(2,1)S(1)}, u32[]{:S(2)}, u32[]{:S(2)}) collective-permute-start(bf16[128,1024]{1,0:T(8,128)(2,1)} %convert_element_type.201), channel_id=1, source_target_pairs={{0,32},{32,64},{64,96},{96,128},{128,160},{160,192},{192,224},{224... | collective-permute-start | bytes 786440 | tf_op jit(solution)/shard_map/while/body/eval_jaxpr/ppermute | solution.py:27
  354.6 2.2 copy-start.8
  354.6 2.2 copy-start.13
  354.6 2.2 copy-start.17
  354.7 2.2 copy-start.20
  354.7 2.2 copy-start.22
  (29 other events, 29.3 us)
Sparse Core Ops, SparseCore 0:
  13.1 75.0 all-gather.1
where the time goes:
time: 366 us; the launch traced here: 365 us
  waiting for transfers between devices  199 us (54%)
  starting transfers between devices  50.6 us (14%)
  other arithmetic  41.9 us (11%)
  local copies, waits for them, and re-layouts  33.2 us (9%)
  matrix products  24.4 us (7%)
  between operations  14.6 us (4%)
    ppermute x17, waiting for transfers between devices, shifted(): lax.ppermute(array, axis, [(i, (i + by) % devices) for i in range(devices)])  143 us
    all_gather x1, waiting for transfers between devices, on_device(): panels = lax.all_gather(keyvals, 'blk', axis=0, tiled=True)  51.1 us
    ppermute x17, starting transfers between devices, shifted(): lax.ppermute(array, axis, [(i, (i + by) % devices) for i in range(devices)])  37.4 us
    add x15, other arithmetic, carry_step(): return running + lax.dynamic_slice_in_dim(far_parts, target * rows, rows, 0)  17.4 us
    ppermute x1, starting transfers between devices, with_halo(): after = lax.ppermute(leading, axis, down)  11.3 us
    convert_element_type x15, other arithmetic, carry_step(): running.astype(jnp.bfloat16)  11.1 us
    while x30, local copies, waits for them, and re-layouts  10.5 us
  transfers between devices with their start and end apart: 20, of which 17 were waited for; matrix products, arithmetic and copies ran while one was open for 10% of the time, Pallas kernels for 0%

commit v1 on v0

--- a/solution.py
+++ b/solution.py
@@ -104,7 +104,9 @@
     values = jnp.dot(normed, w_value, preferred_element_type=f32).astype(bf16)
     keyvals = jnp.concatenate([keys, values], 1)
     window = with_halo(keyvals, (("dom", 0),), rows)
-    panels = lax.all_gather(keyvals, "blk", axis=0, tiled=True)
+    panels = jnp.concatenate(
+        lax.all_to_all(jnp.stack([keyvals] * lax.axis_size("blk")), "blk", 0, 0), axis=0
+    )
     listed = experts_list[0]
     listed_count = listed.shape[0]
     chosen = jnp.take(panels.reshape(groups, rows, 2 * width), listed, axis=0)

time: 366 us -> 352 us (0.962)
  the two profiles are of different devices: /device:TPU:8 before, /device:TPU:16 now
where the time goes in v1:
time: 352 us; the launch traced here: 350 us
  waiting for transfers between devices  187 us (53%)
  starting transfers between devices  64.9 us (18%)
  other arithmetic  38.8 us (11%)
  local copies, waits for them, and re-layouts  34 us (10%)
  matrix products  24 us (7%)
    ppermute x17, waiting for transfers between devices, shifted(): lax.ppermute(array, axis, [(i, (i + by) % devices) for i in range(devices)])  143 us
    ppermute x17, starting transfers between devices, shifted(): lax.ppermute(array, axis, [(i, (i + by) % devices) for i in range(devices)])  43.4 us
    all_to_all x1, waiting for transfers between devices, on_device(): lax.all_to_all(jnp.stack([keyvals] * lax.axis_size('blk')), 'blk', 0, 0)  32.8 us
    add x15, other arithmetic, carry_step(): return running + lax.dynamic_slice_in_dim(far_parts, target * rows, rows, 0)  17.4 us
    convert_element_type x15, other arithmetic, carry_step(): running.astype(jnp.bfloat16)  11.2 us
    while x30, local copies, waits for them, and re-layouts  10.6 us
    all_to_all x1, starting transfers between devices, on_device(): lax.all_to_all(jnp.stack([keyvals] * lax.axis_size('blk')), 'blk', 0, 0)  10.1 us
    ppermute x1, starting transfers between devices, with_halo(): after = lax.ppermute(leading, axis, down)  9.39 us
  transfers between devices with their start and end apart: 20, of which 18 were waited for; matrix products, arithmetic and copies ran while one was open for 9% of the time, Pallas kernels for 0%

profile of v1, /device:TPU:16, one launch (start us, length us, event | category | flops | bytes accessed | tf_op | source)
XLA Modules:
  0.0 350.3 jit_solution(2719347351431978958)
XLA Ops:
  5.7 2.5 stack.2
  8.2 10.1 %all-to-all-start = ((bf16[16,128,1024]{2,1,0:T(8,128)(2,1)}), bf16[16,128,1024]{2,1,0:T(8,128)(2,1)}, u32[]{:S(2)}, u32[]{:S(2)}) async-start(bf16[16,128,1024]{2,1,0:T(8,128)(2,1)} %stack.2), calls=%async_computation | async-start | bytes 8388608 | tf_op jit(solution)/shard_map/all_to_all | solution.py:108
  18.3 9.4 %collective-permute-start.2 = (bf16[128,1024]{1,0:T(8,128)(2,1)S(1)}, bf16[128,1024]{1,0:T(8,128)(2,1)S(1)}, u32[]{:S(2)}, u32[]{:S(2)}) collective-permute-start(bf16[128,1024]{1,0:T(8,128)(2,1)S(1)} %pad_maximum_fusion.2), channel_id=1, source_target_pairs={{1,0},{2,1},{3,2},{4,3},{5,4},{6,5},{7,6},{8,7},{9,8},{10,9},{11,1... | collective-permute-start | bytes 786440 | tf_op jit(solution)/shard_map/ppermute | solution.py:20
  27.7 1.9 collective-permute-start.1
  31.1 7.0 %collective-permute-done.2 = bf16[128,1024]{1,0:T(8,128)(2,1)S(1)} collective-permute-done((bf16[128,1024]{1,0:T(8,128)(2,1)S(1)}, bf16[128,1024]{1,0:T(8,128)(2,1)S(1)}, u32[]{:S(2)}, u32[]{:S(2)}) %collective-permute-start.2) | collective-permute-done | bytes 262176 | tf_op jit(solution)/shard_map/ppermute | solution.py:20
  38.9 3.4 collective-permute-done.1
  43.2 32.8 %all-to-all-done = bf16[16,128,1024]{2,1,0:T(8,128)(2,1)} async-done(((bf16[16,128,1024]{2,1,0:T(8,128)(2,1)}), bf16[16,128,1024]{2,1,0:T(8,128)(2,1)}, u32[]{:S(2)}, u32[]{:S(2)}) %all-to-all-start) | async-done | bytes 4194336 | tf_op jit(solution)/shard_map/all_to_all | solution.py:108
  76.0 2.8 gather_fusion
  86.9 3.7 %fusion.82 = (f32[128]{0:T(128)}, f32[128]{0:T(128)}, f32[128,512]{1,0:T(8,128)}) fusion(f32[128]{0:T(128)} %copy-done.21, f32[128,512]{1,0:T(8,128)S(1)} %get-tuple-element.134, f32[128]{0:T(128)S(1)} %broadcast_multiply_fusion.4, bf16[512,1024]{1,0:T(8,128)(2,1)S(1)} %copy-done, f32[128,1024]{1,0:T(8,128)} %copy-done.16, ...), kind=kOutput, calls=%fused_computation.117 | convolution fusion | flops 271384320 | bytes 3278848 | tf_op jit(solution)/shard_map/dot_general | solution.py:123
  91.8 2.1 convolution_convert_fusion.1
  95.9 3.3 multiply_convert_fusion
  102.4 2.1 fusion.7
  106.3 2.8 copy.26
  114.4 4.9 %copy.28 = f32[16,128,1024]{2,1,0:T(8,128)S(1)} copy(f32[16,128,1024]{2,0,1:T(8,128)S(1)} %fusion.5) | data formatting | bytes 16777216 | tf_op jit(solution)/shard_map/eg,erc->grc/dot_general | solution.py:136
  122.1 12.8 %collective-permute-start.3 = (bf16[128,1024]{1,0:T(8,128)(2,1)}, bf16[128,1024]{1,0:T(8,128)(2,1)}, u32[]{:S(2)}, u32[]{:S(2)}) collective-permute-start(bf16[128,1024]{1,0:T(8,128)(2,1)} %get-tuple-element.127), channel_id=1, source_target_pairs={{0,31},{1,0},{2,1},{3,2},{4,3},{5,4},{6,5},{7,6},{8,7},{9,8},{10,9... | collective-permute-start | bytes 786440 | tf_op jit(solution)/shard_map/ppermute | solution.py:27
  135.0 212.1 %while.15 = (s32[]{:T(128)}, f32[128,1024]{1,0:T(8,128)S(1)}, s32[]{:T(128)}, f32[2048,1024]{1,0:T(8,128)}, s32[]{:T(128)}, /*index=5*/s32[]{:T(128)}, s32[]{:T(...) while((s32[]{:T(128)}, f32[128,1024]{1,0:T(8,128)S(1)}, s32[]{:T(128)}, f32[2048,1024]{1,0:T(8,128)}, ...), condition=%wide.region_10.11_spmd, body=%wide.region_9.10_spmd.sunk | while | flops 393235 | bytes 4194664 | solution.py:144
  135.7 2.0 collective-permute-start
  137.8 9.5 %collective-permute-done = bf16[128,1024]{1,0:T(8,128)(2,1)S(1)} collective-permute-done((bf16[128,1024]{1,0:T(8,128)(2,1)}, bf16[128,1024]{1,0:T(8,128)(2,1)S(1)}, u32[]{:S(2)}, u32[]{:S(2)}) %collective-permute-start) | collective-permute-done | bytes 262176 | tf_op jit(solution)/shard_map/while/body/eval_jaxpr/ppermute | solution.py:27
  151.8 9.6 %collective-permute-done = bf16[128,1024]{1,0:T(8,128)(2,1)S(1)} collective-permute-done((bf16[128,1024]{1,0:T(8,128)(2,1)}, bf16[128,1024]{1,0:T(8,128)(2,1)S(1)}, u32[]{:S(2)}, u32[]{:S(2)}) %collective-permute-start) | collective-permute-done | bytes 262176 | tf_op jit(solution)/shard_map/while/body/eval_jaxpr/ppermute | solution.py:27
  166.0 9.6 %collective-permute-done = bf16[128,1024]{1,0:T(8,128)(2,1)S(1)} collective-permute-done((bf16[128,1024]{1,0:T(8,128)(2,1)}, bf16[128,1024]{1,0:T(8,128)(2,1)S(1)}, u32[]{:S(2)}, u32[]{:S(2)}) %collective-permute-start) | collective-permute-done | bytes 262176 | tf_op jit(solution)/shard_map/while/body/eval_jaxpr/ppermute | solution.py:27
  180.1 9.6 %collective-permute-done = bf16[128,1024]{1,0:T(8,128)(2,1)S(1)} collective-permute-done((bf16[128,1024]{1,0:T(8,128)(2,1)}, bf16[128,1024]{1,0:T(8,128)(2,1)S(1)}, u32[]{:S(2)}, u32[]{:S(2)}) %collective-permute-start) | collective-permute-done | bytes 262176 | tf_op jit(solution)/shard_map/while/body/eval_jaxpr/ppermute | solution.py:27
  194.2 9.6 %collective-permute-done = bf16[128,1024]{1,0:T(8,128)(2,1)S(1)} collective-permute-done((bf16[128,1024]{1,0:T(8,128)(2,1)}, bf16[128,1024]{1,0:T(8,128)(2,1)S(1)}, u32[]{:S(2)}, u32[]{:S(2)}) %collective-permute-start) | collective-permute-done | bytes 262176 | tf_op jit(solution)/shard_map/while/body/eval_jaxpr/ppermute | solution.py:27
  208.4 9.6 %collective-permute-done = bf16[128,1024]{1,0:T(8,128)(2,1)S(1)} collective-permute-done((bf16[128,1024]{1,0:T(8,128)(2,1)}, bf16[128,1024]{1,0:T(8,128)(2,1)S(1)}, u32[]{:S(2)}, u32[]{:S(2)}) %collective-permute-start) | collective-permute-done | bytes 262176 | tf_op jit(solution)/shard_map/while/body/eval_jaxpr/ppermute | solution.py:27
  222.5 9.6 %collective-permute-done = bf16[128,1024]{1,0:T(8,128)(2,1)S(1)} collective-permute-done((bf16[128,1024]{1,0:T(8,128)(2,1)}, bf16[128,1024]{1,0:T(8,128)(2,1)S(1)}, u32[]{:S(2)}, u32[]{:S(2)}) %collective-permute-start) | collective-permute-done | bytes 262176 | tf_op jit(solution)/shard_map/while/body/eval_jaxpr/ppermute | solution.py:27
  236.7 9.6 %collective-permute-done = bf16[128,1024]{1,0:T(8,128)(2,1)S(1)} collective-permute-done((bf16[128,1024]{1,0:T(8,128)(2,1)}, bf16[128,1024]{1,0:T(8,128)(2,1)S(1)}, u32[]{:S(2)}, u32[]{:S(2)}) %collective-permute-start) | collective-permute-done | bytes 262176 | tf_op jit(solution)/shard_map/while/body/eval_jaxpr/ppermute | solution.py:27
  250.8 9.6 %collective-permute-done = bf16[128,1024]{1,0:T(8,128)(2,1)S(1)} collective-permute-done((bf16[128,1024]{1,0:T(8,128)(2,1)}, bf16[128,1024]{1,0:T(8,128)(2,1)S(1)}, u32[]{:S(2)}, u32[]{:S(2)}) %collective-permute-start) | collective-permute-done | bytes 262176 | tf_op jit(solution)/shard_map/while/body/eval_jaxpr/ppermute | solution.py:27
  264.9 9.6 %collective-permute-done = bf16[128,1024]{1,0:T(8,128)(2,1)S(1)} collective-permute-done((bf16[128,1024]{1,0:T(8,128)(2,1)}, bf16[128,1024]{1,0:T(8,128)(2,1)S(1)}, u32[]{:S(2)}, u32[]{:S(2)}) %collective-permute-start) | collective-permute-done | bytes 262176 | tf_op jit(solution)/shard_map/while/body/eval_jaxpr/ppermute | solution.py:27
  279.1 9.6 %collective-permute-done = bf16[128,1024]{1,0:T(8,128)(2,1)S(1)} collective-permute-done((bf16[128,1024]{1,0:T(8,128)(2,1)}, bf16[128,1024]{1,0:T(8,128)(2,1)S(1)}, u32[]{:S(2)}, u32[]{:S(2)}) %collective-permute-start) | collective-permute-done | bytes 262176 | tf_op jit(solution)/shard_map/while/body/eval_jaxpr/ppermute | solution.py:27
  293.2 9.6 %collective-permute-done = bf16[128,1024]{1,0:T(8,128)(2,1)S(1)} collective-permute-done((bf16[128,1024]{1,0:T(8,128)(2,1)}, bf16[128,1024]{1,0:T(8,128)(2,1)S(1)}, u32[]{:S(2)}, u32[]{:S(2)}) %collective-permute-start) | collective-permute-done | bytes 262176 | tf_op jit(solution)/shard_map/while/body/eval_jaxpr/ppermute | solution.py:27
  307.4 9.6 %collective-permute-done = bf16[128,1024]{1,0:T(8,128)(2,1)S(1)} collective-permute-done((bf16[128,1024]{1,0:T(8,128)(2,1)}, bf16[128,1024]{1,0:T(8,128)(2,1)S(1)}, u32[]{:S(2)}, u32[]{:S(2)}) %collective-permute-start) | collective-permute-done | bytes 262176 | tf_op jit(solution)/shard_map/while/body/eval_jaxpr/ppermute | solution.py:27
  321.5 9.6 %collective-permute-done = bf16[128,1024]{1,0:T(8,128)(2,1)S(1)} collective-permute-done((bf16[128,1024]{1,0:T(8,128)(2,1)}, bf16[128,1024]{1,0:T(8,128)(2,1)S(1)}, u32[]{:S(2)}, u32[]{:S(2)}) %collective-permute-start) | collective-permute-done | bytes 262176 | tf_op jit(solution)/shard_map/while/body/eval_jaxpr/ppermute | solution.py:27
  335.6 9.6 %collective-permute-done = bf16[128,1024]{1,0:T(8,128)(2,1)S(1)} collective-permute-done((bf16[128,1024]{1,0:T(8,128)(2,1)}, bf16[128,1024]{1,0:T(8,128)(2,1)S(1)}, u32[]{:S(2)}, u32[]{:S(2)}) %collective-permute-start) | collective-permute-done | bytes 262176 | tf_op jit(solution)/shard_map/while/body/eval_jaxpr/ppermute | solution.py:27
  (183 shorter events, 101.3 us)
Async XLA Ops:
  0.6 84.1 %copy-start = (bf16[512,1024]{1,0:T(8,128)(2,1)S(1)}, bf16[512,1024]{1,0:T(8,128)(2,1)}, u32[]{:S(2)}) copy-start(bf16[512,1024]{1,0:T(8,128)(2,1)} %param.17) | copy-start | bytes 3145732
  8.2 21.5 %copy-start.27 = (s32[1,4]{1,0:T(1,128)S(1)}, s32[1,4]{1,0:T(1,128)}, u32[]{:S(2)}) copy-start(s32[1,4]{1,0:T(1,128)} %param.12) | copy-start | bytes 52
  8.2 21.5 %copy-start.5 = (bf16[128,512]{1,0:T(8,128)(2,1)S(1)}, bf16[128,512]{1,0:T(8,128)(2,1)}, u32[]{:S(2)}) copy-start(bf16[128,512]{1,0:T(8,128)(2,1)} %param.11) | copy-start | bytes 393220
  8.2 21.5 %copy-start.9 = (bf16[512,512]{1,0:T(8,128)(2,1)S(1)}, bf16[512,512]{1,0:T(8,128)(2,1)}, u32[]{:S(2)}) copy-start(bf16[512,512]{1,0:T(8,128)(2,1)} %param.13) | copy-start | bytes 1572868
  8.2 67.9 %all-to-all-start = ((bf16[16,128,1024]{2,1,0:T(8,128)(2,1)}), bf16[16,128,1024]{2,1,0:T(8,128)(2,1)}, u32[]{:S(2)}, u32[]{:S(2)}) async-start(bf16[16,128,1024]{2,1,0:T(8,128)(2,1)} %stack.2), calls=%async_computation | async-start | bytes 8388608 | tf_op jit(solution)/shard_map/all_to_all | solution.py:108
  18.3 19.7 %collective-permute-start.2 = (bf16[128,1024]{1,0:T(8,128)(2,1)S(1)}, bf16[128,1024]{1,0:T(8,128)(2,1)S(1)}, u32[]{:S(2)}, u32[]{:S(2)}) collective-permute-start(bf16[128,1024]{1,0:T(8,128)(2,1)S(1)} %pad_maximum_fusion.2), channel_id=1, source_target_pairs={{1,0},{2,1},{3,2},{4,3},{5,4},{6,5},{7,6},{8,7},{9,8},{10,9},{11,1... | collective-permute-start | bytes 786440 | tf_op jit(solution)/shard_map/ppermute | solution.py:20
  27.7 14.6 %collective-permute-start.1 = (bf16[128,1024]{1,0:T(8,128)(2,1)S(1)}, bf16[128,1024]{1,0:T(8,128)(2,1)S(1)}, u32[]{:S(2)}, u32[]{:S(2)}) collective-permute-start(bf16[128,1024]{1,0:T(8,128)(2,1)S(1)} %pad_maximum_fusion.2), channel_id=1, source_target_pairs={{0,1},{1,2},{2,3},{3,4},{4,5},{5,6},{6,7},{7,8},{8,9},{9,10},{10,1... | collective-permute-start | bytes 786440 | tf_op jit(solution)/shard_map/ppermute | solution.py:19
  82.6 3.3 copy-start.29
  83.6 3.3 copy-start.17
  84.0 7.3 %copy-start.7 = (f32[128,512]{1,0:T(8,128)}, f32[128,512]{1,0:T(8,128)S(1)}, u32[]{:S(2)}) copy-start(f32[128,512]{1,0:T(8,128)S(1)} %get-tuple-element.134) | copy-start | bytes 786436
  99.2 3.2 copy-start.2
  119.3 15.7 %copy-start.4 = (f32[16,128,1024]{2,1,0:T(8,128)}, f32[16,128,1024]{2,1,0:T(8,128)S(1)}, u32[]{:S(2)}) copy-start(f32[16,128,1024]{2,1,0:T(8,128)S(1)} %copy.28) | copy-start | bytes 25165828
  120.2 226.9 %collective-permute-start.4 = (bf16[128,1024]{1,0:T(8,128)(2,1)}, bf16[128,1024]{1,0:T(8,128)(2,1)}, u32[]{:S(2)}, u32[]{:S(2)}) collective-permute-start(bf16[128,1024]{1,0:T(8,128)(2,1)} %get-tuple-element.128), channel_id=1, source_target_pairs={{0,1},{1,2},{2,3},{3,4},{4,5},{5,6},{6,7},{7,8},{8,9},{9,10},{10,1... | collective-permute-start | bytes 786440 | tf_op jit(solution)/shard_map/ppermute | solution.py:27
  122.1 225.0 %collective-permute-start.3 = (bf16[128,1024]{1,0:T(8,128)(2,1)}, bf16[128,1024]{1,0:T(8,128)(2,1)}, u32[]{:S(2)}, u32[]{:S(2)}) collective-permute-start(bf16[128,1024]{1,0:T(8,128)(2,1)} %get-tuple-element.127), channel_id=1, source_target_pairs={{0,31},{1,0},{2,1},{3,2},{4,3},{5,4},{6,5},{7,6},{8,7},{9,8},{10,9... | collective-permute-start | bytes 786440 | tf_op jit(solution)/shard_map/ppermute | solution.py:27
  135.7 11.5 %collective-permute-start = (bf16[128,1024]{1,0:T(8,128)(2,1)}, bf16[128,1024]{1,0:T(8,128)(2,1)S(1)}, u32[]{:S(2)}, u32[]{:S(2)}) collective-permute-start(bf16[128,1024]{1,0:T(8,128)(2,1)} %convert_element_type.201), channel_id=1, source_target_pairs={{0,32},{32,64},{64,96},{96,128},{128,160},{160,192},{192,224},{224... | collective-permute-start | bytes 786440 | tf_op jit(solution)/shard_map/while/body/eval_jaxpr/ppermute | solution.py:27
  149.9 11.5 %collective-permute-start = (bf16[128,1024]{1,0:T(8,128)(2,1)}, bf16[128,1024]{1,0:T(8,128)(2,1)S(1)}, u32[]{:S(2)}, u32[]{:S(2)}) collective-permute-start(bf16[128,1024]{1,0:T(8,128)(2,1)} %convert_element_type.201), channel_id=1, source_target_pairs={{0,32},{32,64},{64,96},{96,128},{128,160},{160,192},{192,224},{224... | collective-permute-start | bytes 786440 | tf_op jit(solution)/shard_map/while/body/eval_jaxpr/ppermute | solution.py:27
  164.0 11.5 %collective-permute-start = (bf16[128,1024]{1,0:T(8,128)(2,1)}, bf16[128,1024]{1,0:T(8,128)(2,1)S(1)}, u32[]{:S(2)}, u32[]{:S(2)}) collective-permute-start(bf16[128,1024]{1,0:T(8,128)(2,1)} %convert_element_type.201), channel_id=1, source_target_pairs={{0,32},{32,64},{64,96},{96,128},{128,160},{160,192},{192,224},{224... | collective-permute-start | bytes 786440 | tf_op jit(solution)/shard_map/while/body/eval_jaxpr/ppermute | solution.py:27
  178.2 11.5 %collective-permute-start = (bf16[128,1024]{1,0:T(8,128)(2,1)}, bf16[128,1024]{1,0:T(8,128)(2,1)S(1)}, u32[]{:S(2)}, u32[]{:S(2)}) collective-permute-start(bf16[128,1024]{1,0:T(8,128)(2,1)} %convert_element_type.201), channel_id=1, source_target_pairs={{0,32},{32,64},{64,96},{96,128},{128,160},{160,192},{192,224},{224... | collective-permute-start | bytes 786440 | tf_op jit(solution)/shard_map/while/body/eval_jaxpr/ppermute | solution.py:27
  192.3 11.5 %collective-permute-start = (bf16[128,1024]{1,0:T(8,128)(2,1)}, bf16[128,1024]{1,0:T(8,128)(2,1)S(1)}, u32[]{:S(2)}, u32[]{:S(2)}) collective-permute-start(bf16[128,1024]{1,0:T(8,128)(2,1)} %convert_element_type.201), channel_id=1, source_target_pairs={{0,32},{32,64},{64,96},{96,128},{128,160},{160,192},{192,224},{224... | collective-permute-start | bytes 786440 | tf_op jit(solution)/shard_map/while/body/eval_jaxpr/ppermute | solution.py:27
  206.4 11.5 %collective-permute-start = (bf16[128,1024]{1,0:T(8,128)(2,1)}, bf16[128,1024]{1,0:T(8,128)(2,1)S(1)}, u32[]{:S(2)}, u32[]{:S(2)}) collective-permute-start(bf16[128,1024]{1,0:T(8,128)(2,1)} %convert_element_type.201), channel_id=1, source_target_pairs={{0,32},{32,64},{64,96},{96,128},{128,160},{160,192},{192,224},{224... | collective-permute-start | bytes 786440 | tf_op jit(solution)/shard_map/while/body/eval_jaxpr/ppermute | solution.py:27
  220.6 11.5 %collective-permute-start = (bf16[128,1024]{1,0:T(8,128)(2,1)}, bf16[128,1024]{1,0:T(8,128)(2,1)S(1)}, u32[]{:S(2)}, u32[]{:S(2)}) collective-permute-start(bf16[128,1024]{1,0:T(8,128)(2,1)} %convert_element_type.201), channel_id=1, source_target_pairs={{0,32},{32,64},{64,96},{96,128},{128,160},{160,192},{192,224},{224... | collective-permute-start | bytes 786440 | tf_op jit(solution)/shard_map/while/body/eval_jaxpr/ppermute | solution.py:27
  234.7 11.5 %collective-permute-start = (bf16[128,1024]{1,0:T(8,128)(2,1)}, bf16[128,1024]{1,0:T(8,128)(2,1)S(1)}, u32[]{:S(2)}, u32[]{:S(2)}) collective-permute-start(bf16[128,1024]{1,0:T(8,128)(2,1)} %convert_element_type.201), channel_id=1, source_target_pairs={{0,32},{32,64},{64,96},{96,128},{128,160},{160,192},{192,224},{224... | collective-permute-start | bytes 786440 | tf_op jit(solution)/shard_map/while/body/eval_jaxpr/ppermute | solution.py:27
  248.9 11.5 %collective-permute-start = (bf16[128,1024]{1,0:T(8,128)(2,1)}, bf16[128,1024]{1,0:T(8,128)(2,1)S(1)}, u32[]{:S(2)}, u32[]{:S(2)}) collective-permute-start(bf16[128,1024]{1,0:T(8,128)(2,1)} %convert_element_type.201), channel_id=1, source_target_pairs={{0,32},{32,64},{64,96},{96,128},{128,160},{160,192},{192,224},{224... | collective-permute-start | bytes 786440 | tf_op jit(solution)/shard_map/while/body/eval_jaxpr/ppermute | solution.py:27
  263.0 11.5 %collective-permute-start = (bf16[128,1024]{1,0:T(8,128)(2,1)}, bf16[128,1024]{1,0:T(8,128)(2,1)S(1)}, u32[]{:S(2)}, u32[]{:S(2)}) collective-permute-start(bf16[128,1024]{1,0:T(8,128)(2,1)} %convert_element_type.201), channel_id=1, source_target_pairs={{0,32},{32,64},{64,96},{96,128},{128,160},{160,192},{192,224},{224... | collective-permute-start | bytes 786440 | tf_op jit(solution)/shard_map/while/body/eval_jaxpr/ppermute | solution.py:27
  277.1 11.5 %collective-permute-start = (bf16[128,1024]{1,0:T(8,128)(2,1)}, bf16[128,1024]{1,0:T(8,128)(2,1)S(1)}, u32[]{:S(2)}, u32[]{:S(2)}) collective-permute-start(bf16[128,1024]{1,0:T(8,128)(2,1)} %convert_element_type.201), channel_id=1, source_target_pairs={{0,32},{32,64},{64,96},{96,128},{128,160},{160,192},{192,224},{224... | collective-permute-start | bytes 786440 | tf_op jit(solution)/shard_map/while/body/eval_jaxpr/ppermute | solution.py:27
  291.3 11.5 %collective-permute-start = (bf16[128,1024]{1,0:T(8,128)(2,1)}, bf16[128,1024]{1,0:T(8,128)(2,1)S(1)}, u32[]{:S(2)}, u32[]{:S(2)}) collective-permute-start(bf16[128,1024]{1,0:T(8,128)(2,1)} %convert_element_type.201), channel_id=1, source_target_pairs={{0,32},{32,64},{64,96},{96,128},{128,160},{160,192},{192,224},{224... | collective-permute-start | bytes 786440 | tf_op jit(solution)/shard_map/while/body/eval_jaxpr/ppermute | solution.py:27
  305.4 11.5 %collective-permute-start = (bf16[128,1024]{1,0:T(8,128)(2,1)}, bf16[128,1024]{1,0:T(8,128)(2,1)S(1)}, u32[]{:S(2)}, u32[]{:S(2)}) collective-permute-start(bf16[128,1024]{1,0:T(8,128)(2,1)} %convert_element_type.201), channel_id=1, source_target_pairs={{0,32},{32,64},{64,96},{96,128},{128,160},{160,192},{192,224},{224... | collective-permute-start | bytes 786440 | tf_op jit(solution)/shard_map/while/body/eval_jaxpr/ppermute | solution.py:27
  319.6 11.5 %collective-permute-start = (bf16[128,1024]{1,0:T(8,128)(2,1)}, bf16[128,1024]{1,0:T(8,128)(2,1)S(1)}, u32[]{:S(2)}, u32[]{:S(2)}) collective-permute-start(bf16[128,1024]{1,0:T(8,128)(2,1)} %convert_element_type.201), channel_id=1, source_target_pairs={{0,32},{32,64},{64,96},{96,128},{128,160},{160,192},{192,224},{224... | collective-permute-start | bytes 786440 | tf_op jit(solution)/shard_map/while/body/eval_jaxpr/ppermute | solution.py:27
  333.7 11.5 %collective-permute-start = (bf16[128,1024]{1,0:T(8,128)(2,1)}, bf16[128,1024]{1,0:T(8,128)(2,1)S(1)}, u32[]{:S(2)}, u32[]{:S(2)}) collective-permute-start(bf16[128,1024]{1,0:T(8,128)(2,1)} %convert_element_type.201), channel_id=1, source_target_pairs={{0,32},{32,64},{64,96},{96,128},{128,160},{160,192},{192,224},{224... | collective-permute-start | bytes 786440 | tf_op jit(solution)/shard_map/while/body/eval_jaxpr/ppermute | solution.py:27
  347.1 2.2 copy-start.8
  347.1 2.2 copy-start.14
  347.2 2.2 copy-start.18
  (32 other events, 34.7 us)
